TPU v7x, 128 devices: a whole 4x4x4 slice. The times are simulated.
128 devices in a mesh: row: 16 (over x, z_hi, core), col: 8 (over y, z_lo).
Axes of the slice: x: 4, y: 4, z: 4 (z_hi: 2, z_lo: 2; z = z_hi * 2 + z_lo), core: 2. Of those that a mesh axis runs over, the one named last changes fastest.
Arguments:
- features: bfloat16 [1024, 128], P(('row', 'col')), may hold values from -6 to 6
- row_weight: bfloat16 [128, 32], replicated, may hold values from -0.5 to 0.5
- col_weight: bfloat16 [128, 32], replicated, may hold values from -0.5 to 0.5
- conv_weight: bfloat16 [2, 9, 64, 64], replicated, may hold values from -0.25 to 0.25
- conv_bias: float32 [2, 64], replicated, may hold values from -3 to 3
- dilations: int32 [2], replicated, may hold values from 1 to 4, as said below
Outputs:
- pair_map: bfloat16 [64, 1024, 1024], P(None, 'row', 'col')
Inputs may be any that keep to these rules, and one draw needn't show every extreme that they name: `dilations`: one dilation a layer; at least one layer uses exactly 4.
All inputs are finite; a program needn't handle non-finite values.
Results may differ from a plain program's by a relative error of at most 0.008.
Values may be sent and summed in bfloat16 or wider, within the bound.
A program may use at most 64 MiB of HBM per device.

v0:
```python
import jax
import jax.numpy as jnp
from jax import lax
from jax.sharding import PartitionSpec as P

MAXDIL = 4


def with_halo(block, sides, width):
    for axis, dim in sides:
        count = lax.axis_size(axis)
        forward = [(i, i + 1) for i in range(count - 1)]
        backward = [(target, source) for source, target in forward]
        low = lax.ppermute(
            lax.slice_in_dim(block, block.shape[dim] - width, None, axis=dim), axis, forward
        )
        high = lax.ppermute(lax.slice_in_dim(block, 0, width, axis=dim), axis, backward)
        block = jnp.concatenate([low, block, high], axis=dim)
    return block


def tap_groups(padded, weights, dilation):
    out_channels = weights.shape[1]
    in_channels = weights.shape[2]
    row_count = padded.shape[1] - 2 * MAXDIL
    col_count = padded.shape[2] - 2 * MAXDIL
    zero_index = jnp.zeros((), jnp.int32)
    dilation = jnp.asarray(dilation)
    summed = jnp.zeros((out_channels, row_count * col_count), jnp.float32)
    for group_index in range(3):
        outer_step = group_index - 1
        pieces = []
        for inner_index in range(3):
            inner_step = inner_index - 1
            row_step, col_step = (outer_step, inner_step)
            row_index = MAXDIL + row_step * dilation
            col_index = MAXDIL + col_step * dilation
            pieces.append(
                lax.dynamic_slice(
                    padded, (zero_index, row_index, col_index), (in_channels, row_count, col_count)
                )
            )
        stacked = jnp.concatenate(pieces, axis=0).reshape(3 * in_channels, row_count * col_count)
        group_weight = jnp.transpose(
            weights[3 * group_index : 3 * group_index + 3], (1, 0, 2)
        ).reshape(out_channels, 3 * in_channels)
        summed = summed + jnp.dot(group_weight, stacked, preferred_element_type=jnp.float32)
    return summed.reshape(out_channels, row_count, col_count)


def finish_layer(pair_now, shift_bias, summed):
    mixed_map = (pair_now.astype(jnp.float32) + shift_bias[:, None, None] + summed).astype(
        jnp.bfloat16
    )
    return lax.optimization_barrier(mixed_map)


def average_pair(mixed_map, mirrored):
    return (0.5 * (mixed_map.astype(jnp.float32) + mirrored.astype(jnp.float32))).astype(
        jnp.bfloat16
    )


def inside_mask(start, count, bins_total):
    places = jnp.arange(count + 2 * MAXDIL) + start - MAXDIL
    return ((places >= 0) & (places < bins_total)).astype(jnp.bfloat16)


def local_start(row_all, col_all, row_start, row_size, col_start, col_size):
    bins_total = row_all.shape[0]
    row_padded = jnp.pad(row_all, ((MAXDIL, MAXDIL), (0, 0)))
    col_padded = jnp.pad(col_all, ((MAXDIL, MAXDIL), (0, 0)))
    row_mask = inside_mask(row_start, row_size, bins_total)
    col_mask = inside_mask(col_start, col_size, bins_total)
    rows_here = lax.dynamic_slice_in_dim(row_padded, row_start, row_size + 2 * MAXDIL, 0)
    cols_here = lax.dynamic_slice_in_dim(col_padded, col_start, col_size + 2 * MAXDIL, 0)
    pair_ext = jnp.concatenate(
        [
            rows_here.T[:, :, None] * col_mask[None, None, :],
            cols_here.T[:, None, :] * row_mask[None, :, None],
        ],
        axis=0,
    )
    rows_across = lax.dynamic_slice_in_dim(row_padded, col_start, col_size + 2 * MAXDIL, 0)
    cols_across = lax.dynamic_slice_in_dim(col_padded, row_start, row_size + 2 * MAXDIL, 0)
    mirror_ext = jnp.concatenate(
        [
            rows_across.T[:, None, :] * row_mask[None, :, None],
            cols_across.T[:, :, None] * col_mask[None, None, :],
        ],
        axis=0,
    )
    return (pair_ext, mirror_ext)


def interior(extended):
    return extended[:, MAXDIL : extended.shape[1] - MAXDIL, MAXDIL : extended.shape[2] - MAXDIL]


def grid_start(row_all, col_all):
    bins_total = row_all.shape[0]
    row_size = bins_total // lax.axis_size("row")
    col_size = bins_total // lax.axis_size("col")
    return local_start(
        row_all,
        col_all,
        lax.axis_index("row") * row_size,
        row_size,
        lax.axis_index("col") * col_size,
        col_size,
    )


def grid_layer(pair_now, padded, layer_weight, shift_bias, dilation):
    if padded is None:
        padded = with_halo(jax.nn.relu(pair_now), (("row", 1), ("col", 2)), MAXDIL)
    summed = tap_groups(padded, layer_weight, dilation)
    mixed_map = finish_layer(pair_now, shift_bias, summed)
    strips = lax.all_to_all(mixed_map, "col", split_axis=1, concat_axis=2, tiled=True)
    turned = lax.all_to_all(
        jnp.swapaxes(strips, 1, 2), ("row", "col"), split_axis=1, concat_axis=2, tiled=True
    )
    mirrored = lax.all_to_all(turned, "col", split_axis=2, concat_axis=1, tiled=True)
    return average_pair(mixed_map, mirrored)


def grid_plan(row_all, col_all, conv_weight, conv_bias, dilations):
    pair_ext, mirror_ext = grid_start(row_all, col_all)
    pair_now = grid_layer(
        interior(pair_ext), jax.nn.relu(pair_ext), conv_weight[0], conv_bias[0], dilations[0]
    )
    pair_now = grid_layer(pair_now, None, conv_weight[1], conv_bias[1], dilations[1])
    return pair_now


def local(features, row_weight, col_weight, conv_weight, conv_bias, dilations):
    row_local = jnp.dot(features, row_weight, preferred_element_type=jnp.float32).astype(
        jnp.bfloat16
    )
    col_local = jnp.dot(features, col_weight, preferred_element_type=jnp.float32).astype(
        jnp.bfloat16
    )
    row_all, col_all = (
        lax.all_gather(row_local, ("row", "col"), axis=0, tiled=True),
        lax.all_gather(col_local, ("row", "col"), axis=0, tiled=True),
    )
    return grid_plan(row_all, col_all, conv_weight, conv_bias, dilations)


def solution(mesh):
    placed = (P(("row", "col"), None), P(), P(), P(), P(), P())
    return jax.shard_map(
        local, mesh=mesh, in_specs=placed, out_specs=P(None, "row", "col"), check_vma=False
    )
```

profile of v0, /device:TPU:0, one launch (start us, length us, event | category | flops | bytes accessed | tf_op | source)
XLA Modules:
  0.0 860.1 jit_solution(7645530848305929042)
XLA Ops:
  4.7 319.4 %all_gather.7 = bf16[1024,32]{1,0:T(8,128)(2,1)S(1)} all-gather(bf16[8,32]{1,0:T(8,128)(2,1)S(1)} %convolution_convert_fusion), channel_id=1, replica_groups=mesh['row'=16,'col'=8] {'row','col'}, dimensions={0}, use_global_device_ids=true | all-gather | bytes 66048 | tf_op jit(solution)/shard_map/all_gather | solution.py:145
  325.1 311.3 %all_gather.6 = bf16[1024,32]{1,0:T(8,128)(2,1)S(1)} all-gather(bf16[8,32]{1,0:T(8,128)(2,1)S(1)} %convolution_convert_fusion.1), channel_id=1, replica_groups=mesh['row'=16,'col'=8] {'row','col'}, dimensions={0}, use_global_device_ids=true | all-gather | bytes 66048 | tf_op jit(solution)/shard_map/all_gather | solution.py:144
  639.6 3.6 constant_dynamic-slice_fusion.10
  647.0 14.7 %all_to_all.90 = bf16[64,64,128]{2,0,1:T(8,128)(2,1)} all-to-all(bf16[64,64,128]{2,0,1:T(8,128)(2,1)S(1)} %fusion.16), channel_id=1, replica_groups=mesh['row'=16,'col'=8] {'col'}, dimensions={1} | all-to-all | bytes 2097152 | tf_op jit(solution)/shard_map/all_to_all | solution.py:119
  666.2 24.7 %all_to_all.91 = bf16[128,2,2048]{2,1,0:T(2,128)(2,1)} all-to-all(bf16[128,2,2048]{2,1,0:T(2,128)(2,1)} %reshape.124), channel_id=1, replica_groups=mesh['row'=16,'col'=8] {'row','col'}, dimensions={0} | all-to-all | bytes 2097152 | tf_op jit(solution)/shard_map/all_to_all | solution.py:120
  690.9 3.8 reshape.125
  696.5 2.7 reshape.126
  699.2 18.4 %all_to_all.92 = bf16[8,2,32768]{2,1,0:T(2,128)(2,1)S(1)} all-to-all(bf16[8,2,32768]{2,1,0:T(2,128)(2,1)} %reshape.126), channel_id=1, replica_groups=mesh['row'=16,'col'=8] {'col'}, dimensions={0} | all-to-all | bytes 2097152 | tf_op jit(solution)/shard_map/all_to_all | solution.py:123
  717.6 2.7 reshape.127
  725.8 4.2 collective-permute-done.1
  734.7 2.7 collective-permute-start.2
  737.4 2.6 copy.58
  745.7 2.9 copy.59
  748.6 2.9 copy.60
  751.5 3.5 pad_maximum_fusion.1
  755.0 6.6 constant_dynamic-slice_fusion.2
  768.4 19.1 %all_to_all.93 = bf16[64,64,128]{2,0,1:T(8,128)(2,1)S(1)} all-to-all(bf16[64,64,128]{2,0,1:T(8,128)(2,1)S(1)} %fusion.15), channel_id=1, replica_groups=mesh['row'=16,'col'=8] {'col'}, dimensions={1} | all-to-all | bytes 2097152 | tf_op jit(solution)/shard_map/all_to_all | solution.py:119
  789.6 3.9 reshape.128
  793.5 28.8 %all_to_all.94 = bf16[128,2,2048]{2,1,0:T(2,128)(2,1)S(1)} all-to-all(bf16[128,2,2048]{2,1,0:T(2,128)(2,1)S(1)} %reshape.128), channel_id=1, replica_groups=mesh['row'=16,'col'=8] {'row','col'}, dimensions={0} | all-to-all | bytes 2097152 | tf_op jit(solution)/shard_map/all_to_all | solution.py:120
  826.6 2.7 copy.117
  829.2 3.4 reshape.130
  832.6 17.8 %all_to_all.95 = bf16[8,2,32768]{2,1,0:T(2,128)(2,1)S(1)} all-to-all(bf16[8,2,32768]{2,1,0:T(2,128)(2,1)S(1)} %reshape.130), channel_id=1, replica_groups=mesh['row'=16,'col'=8] {'col'}, dimensions={0} | all-to-all | bytes 2097152 | tf_op jit(solution)/shard_map/all_to_all | solution.py:123
  850.4 2.7 reshape.131
  853.1 3.4 copy.71
  (77 shorter events, 46.4 us)
Async XLA Ops:
  0.0 3.9 copy-start
  722.7 7.4 copy-start.2
  723.1 6.8 copy-start.4
  723.2 2.6 collective-permute-start
  724.5 5.5 collective-permute-start.1
  734.7 11.0 %collective-permute-start.2 = (bf16[64,72,4]{1,0,2:T(8,128)(2,1)S(1)}, bf16[64,72,4]{1,0,2:T(8,128)(2,1)S(1)}, u32[]{:S(2)}, u32[]{:S(2)}) collective-permute-start(bf16[64,72,4]{1,0,2:T(8,128)(2,1)S(1)} %copy.57), channel_id=1, source_target_pairs={{0,1},{1,2},{2,3},{3,4},{4,5},{5,6},{6,7},{8,9},{9,10},{10,11},{11... | collective-permute-start | bytes 110600 | tf_op jit(solution)/shard_map/ppermute | solution.py:14
  740.0 8.5 collective-permute-start.3
  755.0 6.6 copy-start.13
  761.6 2.5 copy-start.5
  761.6 2.5 copy-start.9
  761.6 2.8 copy-start.10
  761.6 2.8 copy-start.12
  764.4 1.3 copy-start.6
  764.4 1.5 copy-start.7
  764.4 1.9 copy-start.8
  764.4 1.9 copy-start.11
  766.3 1.6 copy-start.3
  853.1 7.1 copy-start.1
where the time goes:
time: 861 us; the launch traced here: 860 us
  blocking collectives  754 us (88%)
  local copies, waits for them, and re-layouts  71.7 us (8%)
  matrix products  9.37 us (1%)
  other arithmetic  8.78 us (1%)
    all_gather x1, blocking collectives, local(): lax.all_gather(col_local, ('row', 'col'), axis=0, tiled=True)  319 us
    all_gather x1, blocking collectives, local(): lax.all_gather(row_local, ('row', 'col'), axis=0, tiled=True)  311 us
    all_to_all x2, blocking collectives, grid_layer(): lax.all_to_all(jnp.swapaxes(strips, 1, 2), ('row', 'col'), split_axis=1,...  53.5 us
    all_to_all x2, blocking collectives, grid_layer(): lax.all_to_all(turned, 'col', split_axis=2, concat_axis=1, tiled=True)  36.2 us
    all_to_all x2, blocking collectives, grid_layer(): lax.all_to_all(mixed_map, 'col', split_axis=1, concat_axis=2, tiled=True)  33.8 us
    unnamed x36, local copies, waits for them, and re-layouts  25 us
  transfers between devices with their start and end apart: 4, of which 1 were waited for; matrix products, arithmetic and copies ran while one was open for 1% of the time, Pallas kernels for 0%

commit v1 on v0

--- a/solution.py
+++ b/solution.py
@@ -140,9 +140,20 @@
     col_local = jnp.dot(features, col_weight, preferred_element_type=jnp.float32).astype(
         jnp.bfloat16
     )
+
+    def guide_pipes(buf):
+        extra = lax.all_to_all(
+            jnp.stack([buf for _ in range(lax.axis_size(("row", "col")))]),
+            axis_name=("row", "col"),
+            split_axis=0,
+            concat_axis=0,
+        )
+        t1 = jnp.concatenate(extra, axis=0)
+        return t1
+
     row_all, col_all = (
         lax.all_gather(row_local, ("row", "col"), axis=0, tiled=True),
-        lax.all_gather(col_local, ("row", "col"), axis=0, tiled=True),
+        guide_pipes(col_local),
     )
     return grid_plan(row_all, col_all, conv_weight, conv_bias, dilations)
 

time: 861 us -> 561 us (0.65)
  blocking collectives: 754 us -> 441 us
  starting transfers between devices: 6.55 us -> 17.7 us
    all_gather x1 -> x0, blocking collectives: 319 us -> none  [local(): lax.all_gather(col_local, ('row', 'col'), axis=0, tiled=True)]
    all_to_all x0 -> x1, starting transfers between devices: none -> 11.2 us  [guide_pipes(): lax.all_to_all(jnp.stack([buf for _ in range(lax.axis_size(('row', 'col')...]
    unnamed x36 -> x38, local copies, waits for them, and re-layouts: 25 us -> 26.5 us
  transfers between devices with their start and end apart: 4 -> 5, of which waited for: 1 -> 1; matrix products, arithmetic and copies ran while one was open for 1% -> 2% of each run, Pallas kernels for 0% -> 0%
where the time goes in v1:
time: 561 us; the launch traced here: 560 us
  blocking collectives  441 us (79%)
  local copies, waits for them, and re-layouts  73.3 us (13%)
  starting transfers between devices  17.7 us (3%)
  matrix products  9.34 us (2%)
  other arithmetic  8.76 us (2%)
    all_gather x1, blocking collectives, local(): lax.all_gather(row_local, ('row', 'col'), axis=0, tiled=True)  318 us
    all_to_all x2, blocking collectives, grid_layer(): lax.all_to_all(jnp.swapaxes(strips, 1, 2), ('row', 'col'), split_axis=1,...  53.5 us
    all_to_all x2, blocking collectives, grid_layer(): lax.all_to_all(turned, 'col', split_axis=2, concat_axis=1, tiled=True)  36.2 us
    all_to_all x2, blocking collectives, grid_layer(): lax.all_to_all(mixed_map, 'col', split_axis=1, concat_axis=2, tiled=True)  33.4 us
    unnamed x38, local copies, waits for them, and re-layouts  26.5 us
  transfers between devices with their start and end apart: 5, of which 1 were waited for; matrix products, arithmetic and copies ran while one was open for 2% of the time, Pallas kernels for 0%

profile of v1, /device:TPU:0, one launch (start us, length us, event | category | flops | bytes accessed | tf_op | source)
XLA Modules:
  0.0 560.2 jit_solution(16438098275071531780)
XLA Ops:
  2.4 11.2 %all-to-all-start = ((bf16[128,2,128]{2,1,0:T(2,128)(2,1)}), bf16[128,2,128]{2,1,0:T(2,128)(2,1)S(1)}, u32[]{:S(2)}, u32[]{:S(2)}) async-start(bf16[128,2,128]{2,1,0:T(2,128)(2,1)} %reshape.130), calls=%async_computation | async-start | bytes 131072 | tf_op jit(solution)/shard_map/all_to_all | solution.py:145
  18.5 318.4 %all_gather.3 = bf16[1024,32]{1,0:T(8,128)(2,1)S(1)} all-gather(bf16[8,32]{1,0:T(8,128)(2,1)S(1)} %convolution_convert_fusion.1), channel_id=1, replica_groups=mesh['row'=16,'col'=8] {'row','col'}, dimensions={0}, use_global_device_ids=true | all-gather | bytes 66048 | tf_op jit(solution)/shard_map/all_gather | solution.py:155
  340.3 3.6 constant_dynamic-slice_fusion.10
  347.7 14.3 %all_to_all.95 = bf16[64,64,128]{2,0,1:T(8,128)(2,1)} all-to-all(bf16[64,64,128]{2,0,1:T(8,128)(2,1)S(1)} %fusion.16), channel_id=1, replica_groups=mesh['row'=16,'col'=8] {'col'}, dimensions={1} | all-to-all | bytes 2097152 | tf_op jit(solution)/shard_map/all_to_all | solution.py:119
  366.4 24.7 %all_to_all.96 = bf16[128,2,2048]{2,1,0:T(2,128)(2,1)} all-to-all(bf16[128,2,2048]{2,1,0:T(2,128)(2,1)} %reshape.132), channel_id=1, replica_groups=mesh['row'=16,'col'=8] {'row','col'}, dimensions={0} | all-to-all | bytes 2097152 | tf_op jit(solution)/shard_map/all_to_all | solution.py:120
  391.1 3.8 reshape.133
  396.6 2.7 reshape.134
  399.3 18.4 %all_to_all.97 = bf16[8,2,32768]{2,1,0:T(2,128)(2,1)S(1)} all-to-all(bf16[8,2,32768]{2,1,0:T(2,128)(2,1)} %reshape.134), channel_id=1, replica_groups=mesh['row'=16,'col'=8] {'col'}, dimensions={0} | all-to-all | bytes 2097152 | tf_op jit(solution)/shard_map/all_to_all | solution.py:123
  417.7 2.7 reshape.135
  425.9 4.2 collective-permute-done.1
  434.9 2.7 collective-permute-start.2
  437.5 2.6 copy.58
  445.8 2.9 copy.59
  448.7 2.9 copy.60
  451.6 3.5 pad_maximum_fusion.1
  455.1 6.6 %constant_dynamic-slice_fusion.2 = (bf16[64,64,128]{2,0,1:T(8,128)(2,1)}, bf16[64,64,128]{2,0,1:T(8,128)(2,1)}, bf16[64,64,128]{2,0,1:T(8,128)(2,1)}, bf16[64,64...) fusion(bf16[64,72,136]{2,0,1:T(8,128)(2,1)S(1)} %pad_maximum_fu, ...), kind=kLoop, calls=%fused_computation.62 | loop fusion | bytes 16777232 | tf_op jit(solution)/shard_map/dynamic_slice | solution.py:39
  468.5 19.1 %all_to_all.98 = bf16[64,64,128]{2,0,1:T(8,128)(2,1)S(1)} all-to-all(bf16[64,64,128]{2,0,1:T(8,128)(2,1)S(1)} %fusion.15), channel_id=1, replica_groups=mesh['row'=16,'col'=8] {'col'}, dimensions={1} | all-to-all | bytes 2097152 | tf_op jit(solution)/shard_map/all_to_all | solution.py:119
  489.7 3.9 reshape.136
  493.6 28.8 %all_to_all.99 = bf16[128,2,2048]{2,1,0:T(2,128)(2,1)S(1)} all-to-all(bf16[128,2,2048]{2,1,0:T(2,128)(2,1)S(1)} %reshape.136), channel_id=1, replica_groups=mesh['row'=16,'col'=8] {'row','col'}, dimensions={0} | all-to-all | bytes 2097152 | tf_op jit(solution)/shard_map/all_to_all | solution.py:120
  526.6 2.7 copy.117
  529.3 3.4 reshape.138
  532.7 17.8 %all_to_all.100 = bf16[8,2,32768]{2,1,0:T(2,128)(2,1)S(1)} all-to-all(bf16[8,2,32768]{2,1,0:T(2,128)(2,1)S(1)} %reshape.138), channel_id=1, replica_groups=mesh['row'=16,'col'=8] {'col'}, dimensions={0} | all-to-all | bytes 2097152 | tf_op jit(solution)/shard_map/all_to_all | solution.py:123
  550.5 2.7 reshape.139
  553.1 3.4 copy.71
  (81 shorter events, 48.0 us)
Async XLA Ops:
  0.0 0.7 copy-start
  2.4 336.9 %all-to-all-start = ((bf16[128,2,128]{2,1,0:T(2,128)(2,1)}), bf16[128,2,128]{2,1,0:T(2,128)(2,1)S(1)}, u32[]{:S(2)}, u32[]{:S(2)}) async-start(bf16[128,2,128]{2,1,0:T(2,128)(2,1)} %reshape.130), calls=%async_computation | async-start | bytes 131072 | tf_op jit(solution)/shard_map/all_to_all | solution.py:145
  422.8 7.4 %copy-start.2 = (f32[64,8,8,128]{3,0,1,2:T(8,128)}, f32[64,8,8,128]{3,0,1,2:T(8,128)S(1)}, u32[]{:S(2)}) copy-start(f32[64,8,8,128]{3,0,1,2:T(8,128)S(1)} %copy.56) | copy-start | bytes 6291460
  423.3 6.8 %copy-start.4 = (bf16[64,64,128]{2,0,1:T(8,128)(2,1)}, bf16[64,64,128]{2,0,1:T(8,128)(2,1)S(1)}, u32[]{:S(2)}) copy-start(bf16[64,64,128]{2,0,1:T(8,128)(2,1)S(1)} %broadcast_maximum_fusion) | copy-start | bytes 3145732
  423.3 2.6 collective-permute-start
  424.6 5.5 collective-permute-start.1
  434.9 10.9 %collective-permute-start.2 = (bf16[64,72,4]{1,0,2:T(8,128)(2,1)S(1)}, bf16[64,72,4]{1,0,2:T(8,128)(2,1)S(1)}, u32[]{:S(2)}, u32[]{:S(2)}) collective-permute-start(bf16[64,72,4]{1,0,2:T(8,128)(2,1)S(1)} %copy.57), channel_id=1, source_target_pairs={{0,1},{1,2},{2,3},{3,4},{4,5},{5,6},{6,7},{8,9},{9,10},{10,11},{11... | collective-permute-start | bytes 110600 | tf_op jit(solution)/shard_map/ppermute | solution.py:14
  440.2 8.5 %collective-permute-start.3 = (bf16[64,72,4]{1,0,2:T(8,128)(2,1)S(1)}, bf16[64,72,4]{1,0,2:T(8,128)(2,1)S(1)}, u32[]{:S(2)}, u32[]{:S(2)}) collective-permute-start(bf16[64,72,4]{1,0,2:T(8,128)(2,1)S(1)} %copy.58), channel_id=1, source_target_pairs={{1,0},{2,1},{3,2},{4,3},{5,4},{6,5},{7,6},{9,8},{10,9},{11,10},{12... | collective-permute-start | bytes 110600 | tf_op jit(solution)/shard_map/ppermute | solution.py:17
  455.1 6.6 %copy-start.13 = (bf16[64,3,64]{0,2,1:T(8,128)(2,1)S(1)}, bf16[64,3,64]{0,2,1:T(8,128)(2,1)}, u32[]{:S(2)}) copy-start(bf16[64,3,64]{0,2,1:T(8,128)(2,1)} %copy.62) | copy-start | bytes 73732
  461.7 2.5 copy-start.5
  461.7 2.5 copy-start.9
  461.7 2.8 copy-start.10
  461.7 2.8 copy-start.12
  464.5 1.3 copy-start.6
  464.5 1.5 copy-start.7
  464.5 1.9 copy-start.8
  464.5 1.9 copy-start.11
  466.4 1.6 copy-start.3
  553.1 7.0 %copy-start.1 = (bf16[128,32]{0,1:T(8,128)(2,1)S(1)}, bf16[128,32]{0,1:T(8,128)(2,1)}, u32[]{:S(2)}) copy-start(bf16[128,32]{0,1:T(8,128)(2,1)} %param.8) | copy-start | bytes 24580
